TPU v7x, 32 devices: a whole 2x2x4 slice. The times are simulated.
32 devices in a mesh: groups: 2 (over x), tensor: 8 (over z, y), dp: 2 (over core).
Axes of the slice: x: 2, y: 2, z: 4, core: 2. Of those that a mesh axis runs over, the one named last changes fastest.
Arguments:
- inputs: bfloat16 [512, 4096], P(('groups', 'tensor', 'dp')), parts along dimension 0, may hold values from -6 to 6
- cotangent: bfloat16 [512, 4096], P(('groups', 'tensor', 'dp')), parts along dimension 0, may hold values from -6 to 6
- gate_blocks: bfloat16 [4096, 8192], P(None, 'tensor'), may hold values from -0.09375 to 0.09375
- gate_scales: float32 [32, 64], P(None, 'tensor'), may hold values from 0.5 to 2
- up_blocks: bfloat16 [4096, 8192], P(None, 'tensor'), may hold values from -0.09375 to 0.09375
- up_scales: float32 [32, 64], P(None, 'tensor'), may hold values from 0.5 to 2
- down_blocks: bfloat16 [8192, 4096], P('tensor'), may hold values from -0.0625 to 0.0625
- down_scales: float32 [64, 32], P('tensor'), may hold values from 0.5 to 2
- first_stored: bfloat16 [8192, 4096], P(None, ('tensor', 'dp')), may hold values from -0.017944336 to 0.017944336
- second_stored: bfloat16 [8192, 4096], P(None, ('tensor', 'dp')), may hold values from 9.953976e-06 to 9.9658966e-05
- owner_map: int32 [16], replicated, may hold values from 0 to 15, each once
Outputs:
- input_grad: bfloat16 [512, 4096], P(('groups', 'tensor', 'dp')), parts along dimension 0
- update: bfloat16 [16384, 4096], P(('groups', 'tensor', 'dp')), parts along dimension 0
There are 2 independent parts, one for each index of `groups`. A program takes and returns all parts, laid end to end along the dimension named above; an argument that names none is the same for every part. Nothing has to cross between parts.
Inputs may be any that keep to these rules, and one draw needn't show every extreme that they name: owner_map is a permutation of the numbers below 16.
All inputs are finite; a program needn't handle non-finite values.
Results may differ from a plain program's by a relative error of at most 0.012.
Values may be sent and summed in bfloat16 or wider, within the bound.
A program may use at most 192 MiB of HBM per device.

v0:
```python
import jax
import jax.numpy as jnp
from jax import lax
from jax.sharding import PartitionSpec as P

BLOCK = 128


def dequantize(blocks, scales, tile):
    rows, cols = blocks.shape
    shaped = blocks.astype(jnp.float32).reshape(rows // tile, tile, cols // tile, tile)
    scaled = shaped * scales[:, None, :, None]
    return scaled.reshape(rows, cols).astype(jnp.bfloat16)


def silu_parts(gate_pre):
    sigma = jax.nn.sigmoid(gate_pre)
    return (gate_pre * sigma, sigma * (1.0 + gate_pre * (1.0 - sigma)))


def reorder(received, placement_of, owner_count):
    rows, cols = received.shape
    shaped = received.reshape(rows, owner_count, cols // owner_count)
    return jnp.take(shaped, placement_of, axis=1).reshape(rows, cols)


def body(
    inputs,
    cotangent,
    gate_blocks,
    gate_scales,
    up_blocks,
    up_scales,
    down_blocks,
    down_scales,
    first_stored,
    second_stored,
    owner_map,
):
    w_gate = dequantize(gate_blocks, gate_scales, BLOCK)
    w_up = dequantize(up_blocks, up_scales, BLOCK)
    w_down = dequantize(down_blocks, down_scales, BLOCK)
    w_both = jnp.concatenate((w_gate, w_up), axis=1)
    units = w_gate.shape[1]
    tok_dev = inputs.shape[0]
    tensor_count = lax.axis_size("tensor")
    dp_count = lax.axis_size("dp")
    rows_all = tok_dev * tensor_count
    mixed = jnp.dot(
        lax.all_gather(inputs, "tensor", axis=0, tiled=True),
        w_both,
        preferred_element_type=jnp.float32,
    )
    gate_pre = mixed[:, :units]
    up_pre = mixed[:, units:]
    activated, slope = silu_parts(gate_pre)
    hidden = (activated * up_pre).astype(jnp.bfloat16)
    piece = lax.all_gather(cotangent, "tensor", axis=0, tiled=True)
    grad_down = lax.dot_general(
        hidden, piece, (((0,), (0,)), ((), ())), preferred_element_type=jnp.float32
    )
    back_rows = lax.dot_general(
        piece, w_down, (((1,), (1,)), ((), ())), preferred_element_type=jnp.float32
    )
    back_hidden = back_rows
    grad_down, back_hidden = (grad_down, back_hidden)
    grad_gate = (back_hidden * up_pre * slope).astype(jnp.bfloat16)
    grad_up = (back_hidden * activated).astype(jnp.bfloat16)
    grad_both = jnp.concatenate((grad_gate, grad_up), axis=1)
    input_grad = lax.psum_scatter(
        lax.dot_general(
            grad_both, w_both, (((1,), (1,)), ((), ())), preferred_element_type=jnp.float32
        ).astype(jnp.bfloat16),
        "tensor",
        scatter_dimension=0,
        tiled=True,
    )
    share = units // dp_count
    summed = lax.psum(grad_down.astype(jnp.bfloat16), "dp").astype(jnp.float32)
    grad_rows = lax.dynamic_slice_in_dim(summed, lax.axis_index("dp") * share, share, 0)
    grad_rows = grad_rows / (rows_all * dp_count)
    owner_count = tensor_count * dp_count
    position = jnp.arange(owner_count, dtype=jnp.int32)
    first_recv, second_recv = (
        lax.all_to_all(first_stored, ("tensor", "dp"), split_axis=0, concat_axis=1, tiled=True),
        lax.all_to_all(second_stored, ("tensor", "dp"), split_axis=0, concat_axis=1, tiled=True),
    )
    target = jnp.take(owner_map, position, axis=0)
    placement_of = jnp.zeros((owner_count,), jnp.int32).at[target].set(position)
    first_true = reorder(first_recv, placement_of, owner_count)
    second_true = reorder(second_recv, placement_of, owner_count)
    first_new = 0.9 * first_true.astype(jnp.float32) + 0.1 * grad_rows
    second_new = 0.95 * second_true.astype(jnp.float32) + 0.05 * grad_rows * grad_rows
    update = (first_new / (jnp.sqrt(second_new) + 1e-08)).astype(jnp.bfloat16)
    return (input_grad, update)


def solution(mesh):
    return jax.shard_map(
        body,
        mesh=mesh,
        in_specs=(
            P(("groups", "tensor", "dp"), None),
            P(("groups", "tensor", "dp"), None),
            P(None, "tensor"),
            P(None, "tensor"),
            P(None, "tensor"),
            P(None, "tensor"),
            P("tensor", None),
            P("tensor", None),
            P(None, ("tensor", "dp")),
            P(None, ("tensor", "dp")),
            P(),
        ),
        out_specs=(P(("groups", "tensor", "dp"), None), P(("groups", "tensor", "dp"), None)),
        check_vma=False,
    )
```

profile of v0, /device:TPU:13, one launch (start us, length us, event | category | flops | bytes accessed | tf_op | source)
XLA Modules:
  0.0 303.1 jit_solution(4564801599368528046)
XLA Ops:
  7.2 0.0 copy-start
  7.2 0.0 copy-start.6
  7.2 0.0 copy-start.7
  7.2 6.7 %all-to-all-start = ((bf16[16,512,256]{2,1,0:T(8,128)(2,1)}), bf16[16,512,256]{2,1,0:T(8,128)(2,1)}, u32[]{:S(2)}, u32[]{:S(2)}) async-start(bf16[16,512,256]{2,1,0:T(8,128)(2,1)} %bitcast.55), calls=%async_computation.1 | async-start | bytes 8388608 | tf_op jit(solution)/shard_map/all_to_all | solution.py:85
  13.9 0.0 all-gather.5.cloned.1.call-start
  13.9 0.7 all-gather.5.cloned.1.call-update
  14.6 0.0 all-gather.3.cloned.1.call-start
  14.6 0.7 all-gather.3.cloned.1.call-update
  15.3 0.0 all-reduce.2.cloned.1.call-start
  15.4 0.0 copy-done.6
  15.4 0.1 copy.16
  15.5 0.0 copy-done.7
  15.5 0.1 copy.15
  15.6 1.1 mul.96
  16.7 6.9 %mul.93 = f32[32,128,8,128]{3,2,1,0:T(8,128)} broadcast(f32[32,8]{1,0:T(8,128)S(1)} %copy.15), dimensions={0,2} | broadcast | bytes 16778240 | tf_op jit(solution)/shard_map/mul | solution.py:12
  23.6 21.3 %fusion = (bf16[4096,1024]{1,0:T(8,128)(2,1)}, bf16[4096,1024]{1,0:T(8,128)(2,1)}) fusion(f32[512,8,8,128]{3,2,1,0:T(8,128)S(1)} %bitcast.51, bf16[4096,1024]{1,0:T(8,128)(2,1)} %param.17, f32[512,8,8,128]{3,2,1,0:T(8,128)} %bitcast.52, bf16[4096,1024]{1,0:T(8,128)(2,1)} %param.15), kind=kLoop, calls=%fused_computation.5 | loop fusion | flops 25165824 | bytes 67108864 | tf_op jit(solution)/shard_map/convert_element_type | solution.py:13
  44.9 51.8 %all-gather.5.cloned.1.call-done = bf16[128,4096]{1,0:T(8,128)(2,1)} async-done(((bf16[16,4096]{1,0:T(8,128)(2,1)}), bf16[128,4096]{1,0:T(8,128)(2,1)}) %all-gather.5.cloned.1.call-update) | async-done | bytes 1048592 | tf_op jit(solution)/shard_map/all_gather | solution.py:50
  96.8 10.8 %fusion.15 = f32[128,2048]{0,1:T(8,128)S(1)} fusion(bf16[128,4096]{1,0:T(8,128)(2,1)} %all-gather.5.cloned.1.call-done, bf16[4096,1024]{1,0:T(8,128)(2,1)} %get-tuple-element.7, bf16[4096,1024]{1,0:T(8,128)(2,1)} %get-tuple-element.8), kind=kOutput, calls=%fused_computation.28 | convolution fusion | flops 2181038080 | bytes 18874368 | tf_op jit(solution)/shard_map/dot_general | solution.py:49
  107.5 0.0 copy-start.4
  107.5 33.1 %all-gather.3.cloned.1.call-done = bf16[128,4096]{1,0:T(8,128)(2,1)} async-done(((bf16[16,4096]{1,0:T(8,128)(2,1)}), bf16[128,4096]{1,0:T(8,128)(2,1)}) %all-gather.3.cloned.1.call-update) | async-done | bytes 1048592 | tf_op jit(solution)/shard_map/all_gather | solution.py:58
  140.6 6.8 %convolution_convert_fusion = bf16[1024,4096]{1,0:T(8,128)(2,1)} fusion(bf16[128,4096]{1,0:T(8,128)(2,1)} %all-gather.3.cloned.1.call-done, f32[128,2048]{0,1:T(8,128)S(1)} %fusion.15), kind=kOutput, calls=%fused_computation.26 | convolution fusion | flops 1078722560 | bytes 10485760 | tf_op jit(solution)/shard_map/dot_general | solution.py:59
  147.5 0.0 copy-start.5
  147.5 0.0 all-reduce.2.cloned.1.call-update
  147.5 0.0 copy-done.4
  147.5 0.0 all-to-all-done
  147.5 7.9 %all-to-all-start.1 = ((bf16[16,512,256]{2,1,0:T(8,128)(2,1)}), bf16[16,512,256]{2,1,0:T(8,128)(2,1)}, u32[]{:S(2)}, u32[]{:S(2)}) async-start(bf16[16,512,256]{2,1,0:T(8,128)(2,1)} %bitcast.56), calls=%async_computation.2 | async-start | bytes 8388608 | tf_op jit(solution)/shard_map/all_to_all | solution.py:86
  155.4 0.0 reduce-scatter.2.cloned.1.call-start
  155.5 0.0 copy-done
  155.5 0.7 gather_fusion
  156.2 0.8 scatter_custom_fusion
  157.1 0.0 copy-done.5
  157.1 0.0 copy-start.3
  157.1 2.2 mul.90
  159.3 0.0 copy-done.3
  159.3 16.7 %multiply_convert_fusion.2 = (bf16[128,1024]{0,1:T(8,128)(2,1)}, bf16[128,1024]{0,1:T(8,128)(2,1)}) fusion(f32[128,2048]{0,1:T(8,128)} %copy-done.4, bf16[128,4096]{1,0:T(8,128)(2,1)S(1)} %copy-done.3, f32[128,8,32,128]{3,2,1,0:T(8,128)S(1)} %bitcast.50, bf16[1024,4096]{1,0:T(8,128)(2,1)} %param.19), kind=kOutput, calls=%fused_computation.35 | convolution fusion | flops 1088028672 | bytes 27787264 | tf_op jit(solution)/shard_map/dot_general | solution.py:62
  176.0 11.6 %fusion.14 = bf16[128,4096]{1,0:T(8,128)(2,1)} fusion(bf16[4096,1024]{1,0:T(8,128)(2,1)} %get-tuple-element.7, bf16[4096,1024]{1,0:T(8,128)(2,1)} %get-tuple-element.8, bf16[128,1024]{0,1:T(8,128)(2,1)} %get-tuple-element.4, bf16[128,1024]{0,1:T(8,128)(2,1)} %get-tuple-element.3), kind=kOutput, calls=%fused_computation.27 | convolution fusion | flops 2182610944 | bytes 18350080 | tf_op jit(solution)/shard_map/dot_general | solution.py:71
  187.6 0.0 reduce-scatter.2.cloned.1.call-update
  187.6 5.0 %gather_fusion.1 = bf16[16,512,256]{2,1,0:T(8,128)(2,1)} fusion(bf16[512,16,256]{2,0,1:T(8,128)(2,1)} %bitcast.5, s32[1024]{0:T(1024)S(1)} %pad_clamp_fusion), kind=kCustom, calls=%fused_computation.clone | custom fusion | bytes 8388672 | tf_op jit(solution)/shard_map/jit(_take)/gather | solution.py:24
  192.6 64.1 %all-to-all-done.1 = bf16[16,512,256]{2,1,0:T(8,128)(2,1)} async-done(((bf16[16,512,256]{2,1,0:T(8,128)(2,1)}), bf16[16,512,256]{2,1,0:T(8,128)(2,1)}, u32[]{:S(2)}, u32[]{:S(2)}) %all-to-all-start.1) | async-done | bytes 4194336 | tf_op jit(solution)/shard_map/all_to_all | solution.py:86
  256.7 4.9 %gather_fusion.2 = bf16[16,512,256]{2,1,0:T(8,128)(2,1)} fusion(bf16[512,16,256]{2,0,1:T(8,128)(2,1)} %bitcast.8, s32[1024]{0:T(1024)S(1)} %pad_clamp_fusion), kind=kCustom, calls=%fused_computation.1.clone | custom fusion | bytes 8388672 | tf_op jit(solution)/shard_map/jit(_take)/gather | solution.py:24
  261.7 11.8 %multiply_bitcast_fusion.1 = (f32[16,64,8,256]{3,2,1,0:T(8,128)}, f32[16,64,8,256]{3,2,1,0:T(8,128)}) fusion(bf16[16,512,256]{2,1,0:T(8,128)(2,1)} %gather_fusion.1, pred[16]{0:T(512)(128)(4,1)S(1)} %compare_and_fusion, bf16[16,512,256]{2,1,0:T(8,128)(2,1)} %gather_fusion.2), kind=kLoop, calls=%fused_computation.24 | loop fusion | flops 12582912 | bytes 25165840
  273.5 0.0 copy-start.2
  273.5 8.1 %copy.20 = f32[16,64,8,256]{3,2,0,1:T(8,128)} copy(f32[16,64,8,256]{3,2,1,0:T(8,128)} %get-tuple-element.6) | data formatting | bytes 16777216 | tf_op jit(solution)/shard_map/mul | solution.py:93
  281.5 0.0 copy-done.2
  281.5 4.2 %copy.19 = f32[16,64,8,256]{3,2,0,1:T(8,128)} copy(f32[16,64,8,256]{3,2,1,0:T(8,128)S(1)} %copy-done.2) | data formatting | bytes 16777216 | tf_op jit(solution)/shard_map/mul | solution.py:92
  285.8 0.0 all-reduce.2.cloned.1.call-done
  285.8 10.7 %fusion.13 = bf16[512,4096]{1,0:T(8,128)(2,1)} fusion(f32[512,4096]{1,0:T(8,128)} %bitcast.53, f32[512,4096]{1,0:T(8,128)} %bitcast.54, bf16[1024,4096]{1,0:T(8,128)(2,1)} %all-reduce.2.cloned.1.call-done, s32[]{:T(128)S(6)} %select_n.35), kind=kLoop, calls=%fused_computation.25 | loop fusion | flops 20971520 | bytes 25165828 | tf_op jit(solution)/shard_map/convert_element_type | solution.py:94
  296.5 0.0 copy-done.1
  (9 shorter events, 0.0 us)
Async XLA Ops:
  7.2 148.3 %copy-start = (s32[16]{0:T(128)S(1)}, s32[16]{0:T(128)}, u32[]{:S(2)}) copy-start(s32[16]{0:T(128)} %param.23) | copy-start | bytes 196
  7.2 8.2 %copy-start.6 = (f32[32,8]{0,1:T(8,128)S(1)}, f32[32,8]{0,1:T(8,128)}, u32[]{:S(2)}) copy-start(f32[32,8]{0,1:T(8,128)} %param.18) | copy-start | bytes 3076
  7.2 8.3 %copy-start.7 = (f32[32,8]{0,1:T(8,128)S(1)}, f32[32,8]{0,1:T(8,128)}, u32[]{:S(2)}) copy-start(f32[32,8]{0,1:T(8,128)} %param.16) | copy-start | bytes 3076
  7.2 140.3 %all-to-all-start = ((bf16[16,512,256]{2,1,0:T(8,128)(2,1)}), bf16[16,512,256]{2,1,0:T(8,128)(2,1)}, u32[]{:S(2)}, u32[]{:S(2)}) async-start(bf16[16,512,256]{2,1,0:T(8,128)(2,1)} %bitcast.55), calls=%async_computation.1 | async-start | bytes 8388608 | tf_op jit(solution)/shard_map/all_to_all | solution.py:85
  13.9 82.9 %all-gather.5.cloned.1.call-start = ((), (), s32[]{:S(2)}) async-start(), calls=%async_computation.4 | async-start | bytes 1179648 | tf_op jit(solution)/shard_map/all_gather | solution.py:50
  14.6 126.0 %all-gather.3.cloned.1.call-start = ((), (), s32[]{:S(2)}) async-start(), calls=%async_computation.3 | async-start | bytes 1179648 | tf_op jit(solution)/shard_map/all_gather | solution.py:58
  15.3 270.4 %all-reduce.2.cloned.1.call-start = ((), (), s32[]{:S(2)}) async-start(), calls=%async_computation.6 | async-start | bytes 16777216 | tf_op jit(solution)/shard_map/psum | solution.py:79
  107.5 40.0 %copy-start.4 = (f32[128,2048]{0,1:T(8,128)}, f32[128,2048]{0,1:T(8,128)S(1)}, u32[]{:S(2)}) copy-start(f32[128,2048]{0,1:T(8,128)S(1)} %fusion.15) | copy-start | bytes 3145732
  147.5 9.6 %copy-start.5 = (f32[8,32]{1,0:T(8,128)S(1)}, f32[8,32]{1,0:T(8,128)}, u32[]{:S(2)}) copy-start(f32[8,32]{1,0:T(8,128)} %param.20) | copy-start | bytes 3076
  147.5 109.2 %all-to-all-start.1 = ((bf16[16,512,256]{2,1,0:T(8,128)(2,1)}), bf16[16,512,256]{2,1,0:T(8,128)(2,1)}, u32[]{:S(2)}, u32[]{:S(2)}) async-start(bf16[16,512,256]{2,1,0:T(8,128)(2,1)} %bitcast.56), calls=%async_computation.2 | async-start | bytes 8388608 | tf_op jit(solution)/shard_map/all_to_all | solution.py:86
  155.4 141.1 %reduce-scatter.2.cloned.1.call-start = ((), (), s32[]{:S(2)}) async-start(), calls=%async_computation.5 | async-start | bytes 1179648 | tf_op jit(solution)/shard_map/reduce_scatter | solution.py:70
  157.1 2.2 copy-start.3
  273.5 8.1 %copy-start.2 = (f32[16,64,8,256]{3,2,1,0:T(8,128)S(1)}, f32[16,64,8,256]{3,2,1,0:T(8,128)}, u32[]{:S(2)}) copy-start(f32[16,64,8,256]{3,2,1,0:T(8,128)} %get-tuple-element.5) | copy-start | bytes 25165828
  285.8 10.8 %copy-start.1 = (s32[16]{0:T(128)S(1)}, s32[16]{0:T(128)}, u32[]{:S(2)}) copy-start(s32[16]{0:T(128)} %param.23) | copy-start | bytes 196
Sparse Core Ops, SparseCore 0:
  16.8 79.9 all-gather.4
  98.9 41.7 all-gather.2
  147.6 39.8 all-reduce.1
  191.4 87.7 reduce-scatter.1
where the time goes:
time: 303 us
  waiting for transfers between devices  150 us (50%)
  matrix products  45.9 us (15%)
  other arithmetic  43.9 us (14%)
  local copies, waits for them, and re-layouts  34.2 us (11%)
  starting transfers between devices  14.7 us (5%)
  between operations  13.9 us (5%)
    all_to_all x1, waiting for transfers between devices, body(): lax.all_to_all(second_stored, ('tensor', 'dp'), split_axis=0, concat_axis...  64.1 us
    all_gather x1, waiting for transfers between devices, body(): lax.all_gather(inputs, 'tensor', axis=0, tiled=True)  51.8 us
    all_gather x1, waiting for transfers between devices, body(): piece = lax.all_gather(cotangent, 'tensor', axis=0, tiled=True)  33.1 us
    convert_element_type x1, other arithmetic, dequantize(): return scaled.reshape(rows, cols).astype(jnp.bfloat16)  21.3 us
    dot_general x1, matrix products, body(): lax.dot_general(piece, w_down, (((1,), (1,)), ((), ())), preferred_elemen...  16.7 us
    unnamed x1, other arithmetic  11.8 us
    dot_general x1, matrix products, body(): lax.dot_general(grad_both, w_both, (((1,), (1,)), ((), ())), preferred_el...  11.6 us
    dot_general x1, matrix products, body(): jnp.dot(lax.all_gather(inputs, 'tensor', axis=0, tiled=True), w_both, pre...  10.8 us
  transfers between devices with their start and end apart: 6, of which 3 were waited for; matrix products, arithmetic and copies ran while one was open for 41% of the time, Pallas kernels for 0%

commit v1 on v0

v1 whole, which is shorter than its diff:
```python
import functools

import jax
import jax.numpy as jnp
from jax import lax
from jax.experimental import pallas as pl
from jax.experimental.pallas import tpu as pltpu
from jax.sharding import PartitionSpec as P

BLOCK = 128
CHUNKS = 4
TOKENS_AXES = ("tensor", "dp")


def dequantize(blocks, scales, tile):
    rows, cols = blocks.shape
    shaped = blocks.astype(jnp.float32).reshape(rows // tile, tile, cols // tile, tile)
    scaled = shaped * scales[:, None, :, None]
    return scaled.reshape(rows, cols).astype(jnp.bfloat16)


def silu_parts(gate_pre):
    sigma = jax.nn.sigmoid(gate_pre)
    return (gate_pre * sigma, sigma * (1.0 + gate_pre * (1.0 - sigma)))


def adam(first, second, grad):
    first_new = 0.9 * first.astype(jnp.float32) + 0.1 * grad
    second_new = 0.95 * second.astype(jnp.float32) + 0.05 * grad * grad
    return (first_new / (jnp.sqrt(second_new) + 1e-08)).astype(jnp.bfloat16)


def adam_kernel(tokens, owner_ref, side_ref, hidden_ref, cot_ref, mine_ref, other_ref, *rest):
    out_ref = rest[-1]
    even = side_ref[0] == 0
    grad = (
        jnp.dot(hidden_ref[...], cot_ref[...], preferred_element_type=jnp.float32) / tokens
    )
    mine = mine_ref[0].astype(jnp.float32)
    other = other_ref[0].astype(jnp.float32)
    first = jnp.where(even, mine, other)
    second = jnp.where(even, other, mine)
    out_ref[...] = adam(first, second, grad)


def adam_chunk(index, chunks, owner_map, side, hidden_t, cot, mine, other, out):
    owners, rows, width = mine.shape
    units, tokens = hidden_t.shape
    cols = cot.shape[1]
    in_specs = [
        pl.BlockSpec((rows, tokens), lambda j, o, s: (index, 0)),
        pl.BlockSpec((tokens, width), lambda j, o, s: (0, o[j])),
        pl.BlockSpec((1, rows, width), lambda j, o, s: (j, 0, 0)),
        pl.BlockSpec((1, rows, width), lambda j, o, s: (j, 0, 0)),
    ]
    args = [owner_map, side, hidden_t, cot, mine, other]
    aliases = {}
    if out is not None:
        in_specs.append(pl.BlockSpec(memory_space=pl.ANY))
        args.append(out)
        aliases = {len(args) - 1: 0}
    return pl.pallas_call(
        functools.partial(adam_kernel, tokens),
        grid_spec=pltpu.PrefetchScalarGridSpec(
            num_scalar_prefetch=2,
            grid=(owners,),
            in_specs=in_specs,
            out_specs=pl.BlockSpec((rows, width), lambda j, o, s: (index, o[j])),
        ),
        out_shape=jax.ShapeDtypeStruct((units, cols), jnp.bfloat16),
        input_output_aliases=aliases,
        cost_estimate=pl.CostEstimate(
            flops=2 * rows * tokens * cols,
            bytes_accessed=2 * rows * cols * 3 + 2 * tokens * cols,
            transcendentals=0,
        ),
        name="adam",
    )(*args)


def body(
    inputs,
    cotangent,
    gate_blocks,
    gate_scales,
    up_blocks,
    up_scales,
    down_blocks,
    down_scales,
    first_stored,
    second_stored,
    owner_map,
):
    group = lax.axis_index("groups")
    half_id = lax.axis_index("dp")
    group_count = lax.axis_size("groups")
    dp_count = lax.axis_size("dp")
    owners = lax.axis_size("tensor") * dp_count
    paired = group_count % 2 == 0
    ff, width = first_stored.shape
    rows = ff // owners
    side = lax.rem(group, 2)

    x_all = lax.all_gather(inputs, TOKENS_AXES, axis=0, tiled=True)
    cot = lax.all_gather(cotangent, TOKENS_AXES, axis=0, tiled=True)

    chunks = CHUNKS if rows % (CHUNKS * 16) == 0 else 1
    step = rows // chunks
    shaped_first = first_stored.reshape(owners, chunks, step, width)
    shaped_second = second_stored.reshape(owners, chunks, step, width)
    swap = [(i, i ^ 1) for i in range(group_count)]
    received = []
    for c in range(chunks):
        if paired:
            picked = jnp.where(side == 0, shaped_first[:, c], shaped_second[:, c])
            mine = lax.all_to_all(picked, TOKENS_AXES, split_axis=0, concat_axis=0, tiled=True)
            received.append((mine, lax.ppermute(mine, "groups", swap)))
        else:
            received.append(
                tuple(
                    lax.all_to_all(a[:, c], TOKENS_AXES, split_axis=0, concat_axis=0, tiled=True)
                    for a in (shaped_first, shaped_second)
                )
            )

    units = gate_blocks.shape[1] // dp_count
    tiles = units // BLOCK
    cut = lambda a, size, dim: lax.dynamic_slice_in_dim(a, half_id * size, size, dim)
    w_gate = dequantize(cut(gate_blocks, units, 1), cut(gate_scales, tiles, 1), BLOCK)
    w_up = dequantize(cut(up_blocks, units, 1), cut(up_scales, tiles, 1), BLOCK)
    w_down = dequantize(cut(down_blocks, units, 0), cut(down_scales, tiles, 0), BLOCK)

    gate_pre = jnp.dot(x_all, w_gate, preferred_element_type=jnp.float32)
    up_pre = jnp.dot(x_all, w_up, preferred_element_type=jnp.float32)
    activated, slope = silu_parts(gate_pre)
    hidden = (activated * up_pre).astype(jnp.bfloat16)
    back_hidden = lax.dot_general(
        cot, w_down, (((1,), (1,)), ((), ())), preferred_element_type=jnp.float32
    )
    grad_gate = (back_hidden * up_pre * slope).astype(jnp.bfloat16)
    grad_up = (back_hidden * activated).astype(jnp.bfloat16)
    nt = (((1,), (1,)), ((), ()))
    partial = lax.dot_general(grad_gate, w_gate, nt, preferred_element_type=jnp.float32)
    partial = partial + lax.dot_general(grad_up, w_up, nt, preferred_element_type=jnp.float32)
    input_grad = lax.psum_scatter(
        partial.astype(jnp.bfloat16), TOKENS_AXES, scatter_dimension=0, tiled=True
    )

    hidden_t = hidden.T
    if width % 128 == 0 and step % 16 == 0:
        sides = jnp.full((1,), side if paired else 0, jnp.int32)
        update = None
        for c, (mine, other) in enumerate(received):
            update = adam_chunk(
                c, chunks, owner_map, sides, hidden_t, cot, mine, other, update
            )
    else:
        grad = jnp.dot(hidden_t, cot, preferred_element_type=jnp.float32) / cot.shape[0]
        placement = jnp.zeros((owners,), jnp.int32).at[owner_map].set(
            jnp.arange(owners, dtype=jnp.int32)
        )
        parts = []
        for c, (mine, other) in enumerate(received):
            if paired:
                first = jnp.where(side == 0, mine, other)
                second = jnp.where(side == 0, other, mine)
            else:
                first, second = mine, other
            lay = lambda a: jnp.take(a, placement, axis=0).swapaxes(0, 1).reshape(step, -1)
            parts.append(adam(lay(first), lay(second), grad[c * step : (c + 1) * step]))
        update = jnp.concatenate(parts, axis=0)
    return (input_grad, update)


def solution(mesh):
    return jax.shard_map(
        body,
        mesh=mesh,
        in_specs=(
            P(("groups", "tensor", "dp"), None),
            P(("groups", "tensor", "dp"), None),
            P(None, "tensor"),
            P(None, "tensor"),
            P(None, "tensor"),
            P(None, "tensor"),
            P("tensor", None),
            P("tensor", None),
            P(None, ("tensor", "dp")),
            P(None, ("tensor", "dp")),
            P(),
        ),
        out_specs=(P(("groups", "tensor", "dp"), None), P(("groups", "tensor", "dp"), None)),
        check_vma=False,
    )
```

time: 303 us -> 249 us (0.82); the launches traced: 303 us -> 245 us
  Pallas kernels: 0 us -> 48.6 us
  waiting for transfers between devices: 150 us -> 111 us
  local copies, waits for them, and re-layouts: 34.2 us -> 4.83 us
  other arithmetic: 43.9 us -> 17.3 us
  matrix products: 45.9 us -> 21.7 us
  starting transfers between devices: 14.7 us -> 27.2 us
    all_gather x2, waiting for transfers between devices: 84.9 us -> 12.4 us  [the longest x1 12.4 us: body(): cot = lax.all_gather(cotangent, TOKENS_AXES, axis=0, tiled=True)]
    pallas_call x0 -> x4, Pallas kernels: none -> 48.6 us  [adam_chunk(): pl.pallas_call(functools.partial(adam_kernel, tokens), grid_spec=pltpu.Pr...]
    ppermute x0 -> x4, waiting for transfers between devices: none -> 26.5 us  [body(): received.append((mine, lax.ppermute(mine, 'groups', swap)))]
    dot_general x4 -> x5, matrix products: 45.9 us -> 21.7 us  [the longest x1 7.42 us: body(): lax.dot_general(cot, w_down, (((1,), (1,)), ((), ())), preferred_element_...]
    mul x2 -> x0, local copies, waits for them, and re-layouts: 12.3 us -> none  [the longest x1 8.06 us: body(): 0.95 * second_true.astype(jnp.float32) + 0.05 * grad_rows * grad_rows]
    unnamed x1 -> x0, other arithmetic: 11.8 us -> none
    convert_element_type x1 -> x0, other arithmetic: 10.7 us -> none  [body(): update = (first_new / (jnp.sqrt(second_new) + 1e-08)).astype(jnp.bfloat16)]
    gather x3 -> x0, local copies, waits for them, and re-layouts: 10.6 us -> none  [the longest x2 9.96 us: reorder(): return jnp.take(shaped, placement_of, axis=1).reshape(rows, cols)]
  transfers between devices with their start and end apart: 6 -> 11, of which waited for: 3 -> 7; matrix products, arithmetic and copies ran while one was open for 41% -> 17% of each run, Pallas kernels for 0% -> 20%
where the time goes in v1:
time: 249 us; the launch traced here: 245 us
  waiting for transfers between devices  111 us (45%)
  Pallas kernels  48.6 us (20%)
  starting transfers between devices  27.2 us (11%)
  matrix products  21.7 us (9%)
  other arithmetic  17.3 us (7%)
  between operations  13.9 us (6%)
  local copies, waits for them, and re-layouts  4.83 us (2%)
    all_to_all x4, waiting for transfers between devices, body(): lax.all_to_all(picked, TOKENS_AXES, split_axis=0, concat_axis=0, tiled=True)  71.2 us
    pallas_call x4, Pallas kernels, adam_chunk(): pl.pallas_call(functools.partial(adam_kernel, tokens), grid_spec=pltpu.Pr...  48.6 us
    ppermute x4, waiting for transfers between devices, body(): received.append((mine, lax.ppermute(mine, 'groups', swap)))  26.5 us
    all_to_all x4, starting transfers between devices, body(): lax.all_to_all(picked, TOKENS_AXES, split_axis=0, concat_axis=0, tiled=True)  23.1 us
    all_gather x1, waiting for transfers between devices, body(): cot = lax.all_gather(cotangent, TOKENS_AXES, axis=0, tiled=True)  12.4 us
    convert_element_type x2, other arithmetic, dequantize(): return scaled.reshape(rows, cols).astype(jnp.bfloat16)  11.8 us
    dot_general x1, matrix products, body(): lax.dot_general(cot, w_down, (((1,), (1,)), ((), ())), preferred_element_...  7.42 us
    select_n x1, other arithmetic, body(): picked = jnp.where(side == 0, shaped_first[:, c], shaped_second[:, c])  5.45 us
  transfers between devices with their start and end apart: 11, of which 7 were waited for; matrix products, arithmetic and copies ran while one was open for 17% of the time, Pallas kernels for 20%

profile of v1, /device:TPU:13, one launch (start us, length us, event | category | flops | bytes accessed | tf_op | source)
XLA Modules:
  0.0 245.0 jit_solution(3878550512586177357)
XLA Ops:
  7.2 0.0 copy-start
  7.2 0.0 all-gather.5.cloned.1.call-start
  7.2 0.7 all-gather.5.cloned.1.call-update
  7.9 0.0 copy-start.10
  7.9 0.0 copy-start.11
  7.9 5.5 %fusion.11 = (bf16[16,128,256]{2,1,0:T(8,128)(2,1)}, bf16[16,128,256]{2,1,0:T(8,128)(2,1)}, bf16[16,128,256]{2,1,0:T(8,128)(2,1)}, bf16[16,128,256]{2,1,0:T(8,128)(2,1)}) fusion(bf16[16,4,128,256]{3,2,1,0:T(8,128)(2,1)} %bitcast.117, bf16[16,4,128,256]{3,2,1,0:T(8,128)(2,1)} %bitcast.118, pred[]{:T(512)S(6)} %eq.2), kind=kLoop, calls=%fused_computation.13 | loop fusion | flops 2097152 | bytes 12582913 | tf_op jit(solution)/shard_map/jit(_where)/select_n | solution.py:115
  13.4 6.5 %all-to-all-start.1 = ((bf16[16,128,256]{2,1,0:T(8,128)(2,1)}), bf16[16,128,256]{2,1,0:T(8,128)(2,1)S(1)}, u32[]{:S(2)}, u32[]{:S(2)}) async-start(bf16[16,128,256]{2,1,0:T(8,128)(2,1)} %get-tuple-element.4), calls=%async_computation.2 | async-start | bytes 2097152 | tf_op jit(solution)/shard_map/all_to_all | solution.py:116
  19.9 0.0 all-gather.3.cloned.1.call-start
  20.0 0.7 all-gather.3.cloned.1.call-update
  20.7 0.0 copy-done.10
  20.7 0.0 copy-done.11
  20.7 0.1 copy.19
  20.8 36.4 %all-to-all-done.1.mine_ref = bf16[16,128,256]{2,1,0:T(8,128)(2,1)S(1)} async-done(((bf16[16,128,256]{2,1,0:T(8,128)(2,1)}), bf16[16,128,256]{2,1,0:T(8,128)(2,1)S(1)}, u32[]{:S(2)}, u32[]{:S(2)}) %all-to-all-start.1) | async-done | bytes 1048608 | tf_op jit(solution)/shard_map/all_to_all | solution.py:116
  57.2 4.2 %all-to-all-start.2 = ((bf16[16,128,256]{2,1,0:T(8,128)(2,1)}), bf16[16,128,256]{2,1,0:T(8,128)(2,1)S(1)}, u32[]{:S(2)}, u32[]{:S(2)}) async-start(bf16[16,128,256]{2,1,0:T(8,128)(2,1)} %get-tuple-element.3), calls=%async_computation.3 | async-start | bytes 2097152 | tf_op jit(solution)/shard_map/all_to_all | solution.py:116
  61.4 1.1 mul.77
  62.5 5.9 %fusion = bf16[4096,512]{1,0:T(8,128)(2,1)} fusion(f32[512,8,4,128]{3,2,1,0:T(4,128)S(1)} %bitcast.115, bf16[4096,1024]{1,0:T(8,128)(2,1)} %param.13, s32[]{:T(128)S(6)} %select_n.42), kind=kLoop, calls=%fused_computation.1 | loop fusion | flops 6291456 | bytes 16777220 | tf_op jit(solution)/shard_map/convert_element_type | solution.py:19
  68.5 0.1 copy.18
  68.6 1.1 mul.73
  69.7 5.9 %fusion.1 = bf16[4096,512]{1,0:T(8,128)(2,1)} fusion(f32[512,8,4,128]{3,2,1,0:T(4,128)S(1)} %bitcast.116, bf16[4096,1024]{1,0:T(8,128)(2,1)} %param.15, s32[]{:T(128)S(6)} %select_n.42), kind=kLoop, calls=%fused_computation.3 | loop fusion | flops 6291456 | bytes 16777220 | tf_op jit(solution)/shard_map/convert_element_type | solution.py:19
  75.6 5.0 %fusion.35 = f32[512,256]{1,0:T(8,128)} fusion(bf16[4096,512]{1,0:T(8,128)(2,1)} %fusion, bf16[256,4096]{1,0:T(8,128)(2,1)} %all-gather.5.cloned.1.call-done), kind=kOutput, calls=%fused_computation.50 | convolution fusion | flops 1073741824 | bytes 6815744 | tf_op jit(solution)/shard_map/dot_general | solution.py:133
  80.7 9.8 %all-to-all-done.2.mine_ref = bf16[16,128,256]{2,1,0:T(8,128)(2,1)S(1)} async-done(((bf16[16,128,256]{2,1,0:T(8,128)(2,1)}), bf16[16,128,256]{2,1,0:T(8,128)(2,1)S(1)}, u32[]{:S(2)}, u32[]{:S(2)}) %all-to-all-start.2) | async-done | bytes 1048608 | tf_op jit(solution)/shard_map/all_to_all | solution.py:116
  90.5 4.8 %all-to-all-start.3 = ((bf16[16,128,256]{2,1,0:T(8,128)(2,1)}), bf16[16,128,256]{2,1,0:T(8,128)(2,1)S(1)}, u32[]{:S(2)}, u32[]{:S(2)}) async-start(bf16[16,128,256]{2,1,0:T(8,128)(2,1)} %get-tuple-element.2), calls=%async_computation.4 | async-start | bytes 2097152 | tf_op jit(solution)/shard_map/all_to_all | solution.py:116
  95.3 0.2 reduce-scatter.2.cloned.1.call-start
  95.5 5.1 %multiply_convert_fusion = (bf16[512,256]{1,0:T(8,128)(2,1)}, f32[512,256]{1,0:T(8,128)}) fusion(f32[512,256]{1,0:T(8,128)} %fusion.35, bf16[4096,512]{1,0:T(8,128)(2,1)} %fusion.1, bf16[256,4096]{1,0:T(8,128)(2,1)} %all-gather.5.cloned.1.call-done), kind=kOutput, calls=%fused_computation.40 | convolution fusion | flops 1074528256 | bytes 7602176 | tf_op jit(solution)/shard_map/dot_general | solution.py:134
  100.7 12.4 %all-gather.3.cloned.1.call-done.cot_ref = bf16[256,4096]{1,0:T(8,128)(2,1)} async-done(((bf16[16,4096]{1,0:T(8,128)(2,1)}), bf16[256,4096]{1,0:T(8,128)(2,1)}) %all-gather.3.cloned.1.call-update) | async-done | bytes 2097168 | tf_op jit(solution)/shard_map/all_gather | solution.py:105
  113.0 1.1 mul.70
  114.2 0.5 copy-done.2
  114.6 7.4 %fusion.7 = f32[256,512]{0,1:T(8,128)S(1)} fusion(bf16[256,4096]{1,0:T(8,128)(2,1)S(1)} %copy-done.2, f32[64,8,32,128]{3,2,1,0:T(8,128)S(1)} %bitcast.114, bf16[1024,4096]{1,0:T(8,128)(2,1)} %param.17, s32[]{:T(128)S(6)} %select_n.42), kind=kOutput, calls=%fused_computation.10 | convolution fusion | flops 1080033280 | bytes 15204356 | tf_op jit(solution)/shard_map/dot_general | solution.py:137
  122.1 1.4 fusion.28
  123.6 0.7 copy-done.4
  124.3 2.7 %fusion.3 = bf16[256,4096]{1,0:T(8,128)(2,1)} fusion(f32[256,4096]{1,0:T(8,128)S(1)} %fusion.28, bf16[4096,512]{1,0:T(8,128)(2,1)S(1)} %copy-done.4, f32[256,512]{0,1:T(8,128)S(1)} %fusion.7, f32[512,256]{1,0:T(8,128)S(1)} %copy-done.8), kind=kOutput, calls=%fused_computation.7 | convolution fusion | flops 1076625408 | bytes 11534336 | tf_op jit(solution)/shard_map/dot_general | solution.py:144
  127.0 0.0 reduce-scatter.2.cloned.1.call-update
  127.0 0.0 all-to-all-done.3.mine_ref
  127.0 7.5 %all-to-all-start = ((bf16[16,128,256]{2,1,0:T(8,128)(2,1)}), bf16[16,128,256]{2,1,0:T(8,128)(2,1)}, u32[]{:S(2)}, u32[]{:S(2)}) async-start(bf16[16,128,256]{2,1,0:T(8,128)(2,1)} %get-tuple-element.5), calls=%async_computation.1 | async-start | bytes 2097152 | tf_op jit(solution)/shard_map/all_to_all | solution.py:116
  134.5 1.2 collective-permute-start.3
  135.7 0.3 collective-permute-start.2
  136.0 1.2 collective-permute-start.1
  137.2 25.0 %all-to-all-done.mine_ref = bf16[16,128,256]{2,1,0:T(8,128)(2,1)} async-done(((bf16[16,128,256]{2,1,0:T(8,128)(2,1)}), bf16[16,128,256]{2,1,0:T(8,128)(2,1)}, u32[]{:S(2)}, u32[]{:S(2)}) %all-to-all-start) | async-done | bytes 1048608 | tf_op jit(solution)/shard_map/all_to_all | solution.py:116
  162.2 1.2 collective-permute-start
  163.3 0.0 collective-permute-done.3.other_ref
  163.3 12.1 %adam.4.rest_0_ = bf16[512,4096]{1,0:T(8,128)(2,1)} custom-call(s32[16]{0:T(128)} %owner_ref.7, s32[1]{0:T(128)} %bitcast.3.side_ref, bf16[512,256]{1,0:T(8,128)(2,1)} %get-tuple-element.6.hidden_ref, bf16[256,4096]{1,0:T(8,128)(2,1)} %all-gather.3.cloned.1.call-done.cot_ref, bf16[16,128,256]{2,1,0:T(8,128)(2,1)} %copy-done.7, ...), custom_call_target="tpu_custom_call" | custom-call | flops 268435456 | bytes 5242880 | tf_op jit(solution)/shard_map/adam/pallas_call | solution.py:62
  175.5 5.9 %collective-permute-done.2.other_ref = bf16[16,128,256]{2,1,0:T(8,128)(2,1)} collective-permute-done((bf16[16,128,256]{2,1,0:T(8,128)(2,1)S(1)}, bf16[16,128,256]{2,1,0:T(8,128)(2,1)}, u32[]{:S(2)}, u32[]{:S(2)}) %collective-permute-start.2) | collective-permute-done | bytes 1048608 | tf_op jit(solution)/shard_map/ppermute | solution.py:117
  181.4 12.1 %adam.5.rest_0_ = bf16[512,4096]{1,0:T(8,128)(2,1)} custom-call(s32[16]{0:T(128)} %owner_ref.7, s32[1]{0:T(128)} %bitcast.3.side_ref, bf16[512,256]{1,0:T(8,128)(2,1)} %get-tuple-element.6.hidden_ref, bf16[256,4096]{1,0:T(8,128)(2,1)} %all-gather.3.cloned.1.call-done.cot_ref, bf16[16,128,256]{2,1,0:T(8,128)(2,1)} %copy-done.6, ...), custom_call_target="tpu_custom_call", output_to_operand_aliasing={{}: (6, {})} | custom-call | flops 268435456 | bytes 5242880 | tf_op jit(solution)/shard_map/adam/pallas_call | solution.py:62
  193.5 10.3 %collective-permute-done.1.other_ref = bf16[16,128,256]{2,1,0:T(8,128)(2,1)} collective-permute-done((bf16[16,128,256]{2,1,0:T(8,128)(2,1)S(1)}, bf16[16,128,256]{2,1,0:T(8,128)(2,1)}, u32[]{:S(2)}, u32[]{:S(2)}) %collective-permute-start.1) | collective-permute-done | bytes 1048608 | tf_op jit(solution)/shard_map/ppermute | solution.py:117
  203.9 12.2 %adam.6.rest_0_ = bf16[512,4096]{1,0:T(8,128)(2,1)} custom-call(s32[16]{0:T(128)} %owner_ref.7, s32[1]{0:T(128)} %bitcast.3.side_ref, bf16[512,256]{1,0:T(8,128)(2,1)} %get-tuple-element.6.hidden_ref, bf16[256,4096]{1,0:T(8,128)(2,1)} %all-gather.3.cloned.1.call-done.cot_ref, bf16[16,128,256]{2,1,0:T(8,128)(2,1)} %copy-done.5, ...), custom_call_target="tpu_custom_call", output_to_operand_aliasing={{}: (6, {})} | custom-call | flops 268435456 | bytes 5242880 | tf_op jit(solution)/shard_map/adam/pallas_call | solution.py:62
  216.1 10.2 %collective-permute-done.other_ref = bf16[16,128,256]{2,1,0:T(8,128)(2,1)} collective-permute-done((bf16[16,128,256]{2,1,0:T(8,128)(2,1)}, bf16[16,128,256]{2,1,0:T(8,128)(2,1)}, u32[]{:S(2)}, u32[]{:S(2)}) %collective-permute-start) | collective-permute-done | bytes 1048608 | tf_op jit(solution)/shard_map/ppermute | solution.py:117
  226.3 12.1 %adam.7 = bf16[512,4096]{1,0:T(8,128)(2,1)} custom-call(s32[16]{0:T(128)} %owner_ref.7, s32[1]{0:T(128)} %bitcast.3.side_ref, bf16[512,256]{1,0:T(8,128)(2,1)} %get-tuple-element.6.hidden_ref, bf16[256,4096]{1,0:T(8,128)(2,1)} %all-gather.3.cloned.1.call-done.cot_ref, bf16[16,128,256]{2,1,0:T(8,128)(2,1)} %all-to-all-done.mine_ref, ...), custom_call_target="tpu_custom_call", output_to_operand_aliasing={{}: (6, {})} | custom-call | flops 268435456 | bytes 5242880 | tf_op jit(solution)/shard_map/adam/pallas_call | solution.py:62
  238.5 0.0 copy-done.1
  (20 shorter events, 0.0 us)
Async XLA Ops:
  7.2 61.4 %copy-start = (f32[8,32]{1,0:T(8,128)S(1)}, f32[8,32]{1,0:T(8,128)}, u32[]{:S(2)}) copy-start(f32[8,32]{1,0:T(8,128)} %param.18) | copy-start | bytes 3076
  7.2 68.5 %all-gather.5.cloned.1.call-start = ((), (), s32[]{:S(2)}) async-start(), calls=%async_computation.6 | async-start | bytes 2228224 | tf_op jit(solution)/shard_map/all_gather | solution.py:104
  7.9 12.8 %copy-start.10 = (f32[32,8]{0,1:T(8,128)S(1)}, f32[32,8]{0,1:T(8,128)}, u32[]{:S(2)}) copy-start(f32[32,8]{0,1:T(8,128)} %param.14) | copy-start | bytes 3076
  7.9 12.8 %copy-start.11 = (f32[32,8]{0,1:T(8,128)S(1)}, f32[32,8]{0,1:T(8,128)}, u32[]{:S(2)}) copy-start(f32[32,8]{0,1:T(8,128)} %param.16) | copy-start | bytes 3076
  13.4 43.8 %all-to-all-start.1 = ((bf16[16,128,256]{2,1,0:T(8,128)(2,1)}), bf16[16,128,256]{2,1,0:T(8,128)(2,1)S(1)}, u32[]{:S(2)}, u32[]{:S(2)}) async-start(bf16[16,128,256]{2,1,0:T(8,128)(2,1)} %get-tuple-element.4), calls=%async_computation.2 | async-start | bytes 2097152 | tf_op jit(solution)/shard_map/all_to_all | solution.py:116
  19.9 93.1 %all-gather.3.cloned.1.call-start = ((), (), s32[]{:S(2)}) async-start(), calls=%async_computation.5 | async-start | bytes 2228224 | tf_op jit(solution)/shard_map/all_gather | solution.py:105
  57.2 78.8 %copy-start.5 = (bf16[16,128,256]{2,1,0:T(8,128)(2,1)}, bf16[16,128,256]{2,1,0:T(8,128)(2,1)S(1)}, u32[]{:S(2)}) copy-start(bf16[16,128,256]{2,1,0:T(8,128)(2,1)S(1)} %all-to-all-done.1.mine_ref) | copy-start | bytes 3145732
  57.2 33.3 %all-to-all-start.2 = ((bf16[16,128,256]{2,1,0:T(8,128)(2,1)}), bf16[16,128,256]{2,1,0:T(8,128)(2,1)S(1)}, u32[]{:S(2)}, u32[]{:S(2)}) async-start(bf16[16,128,256]{2,1,0:T(8,128)(2,1)} %get-tuple-element.3), calls=%async_computation.3 | async-start | bytes 2097152 | tf_op jit(solution)/shard_map/all_to_all | solution.py:116
  90.5 45.2 %copy-start.6 = (bf16[16,128,256]{2,1,0:T(8,128)(2,1)}, bf16[16,128,256]{2,1,0:T(8,128)(2,1)S(1)}, u32[]{:S(2)}) copy-start(bf16[16,128,256]{2,1,0:T(8,128)(2,1)S(1)} %all-to-all-done.2.mine_ref) | copy-start | bytes 3145732
  90.5 36.6 %all-to-all-start.3 = ((bf16[16,128,256]{2,1,0:T(8,128)(2,1)}), bf16[16,128,256]{2,1,0:T(8,128)(2,1)S(1)}, u32[]{:S(2)}, u32[]{:S(2)}) async-start(bf16[16,128,256]{2,1,0:T(8,128)(2,1)} %get-tuple-element.2), calls=%async_computation.4 | async-start | bytes 2097152 | tf_op jit(solution)/shard_map/all_to_all | solution.py:116
  95.3 143.2 %reduce-scatter.2.cloned.1.call-start = ((), (), s32[]{:S(2)}) async-start(), calls=%async_computation.7 | async-start | bytes 2228224 | tf_op jit(solution)/shard_map/reduce_scatter | solution.py:145
  113.0 1.6 copy-start.2
  114.6 7.4 %copy-start.3 = (bf16[4096,512]{1,0:T(8,128)(2,1)S(1)}, bf16[4096,512]{1,0:T(8,128)(2,1)}, u32[]{:S(2)}) copy-start(bf16[4096,512]{1,0:T(8,128)(2,1)} %fusion) | copy-start | bytes 12582916
  114.6 7.4 %copy-start.8 = (f32[512,256]{1,0:T(8,128)S(1)}, f32[512,256]{1,0:T(8,128)}, u32[]{:S(2)}) copy-start(f32[512,256]{1,0:T(8,128)} %fusion.35) | copy-start | bytes 1572868
  114.6 7.5 %copy-start.9 = (f32[512,256]{1,0:T(8,128)S(1)}, f32[512,256]{1,0:T(8,128)}, u32[]{:S(2)}) copy-start(f32[512,256]{1,0:T(8,128)} %get-tuple-element.7) | copy-start | bytes 1572868
  122.1 2.2 copy-start.4
  127.0 36.3 %copy-start.7 = (bf16[16,128,256]{2,1,0:T(8,128)(2,1)}, bf16[16,128,256]{2,1,0:T(8,128)(2,1)S(1)}, u32[]{:S(2)}) copy-start(bf16[16,128,256]{2,1,0:T(8,128)(2,1)S(1)} %all-to-all-done.3.mine_ref) | copy-start | bytes 3145732
  127.0 35.1 %all-to-all-start = ((bf16[16,128,256]{2,1,0:T(8,128)(2,1)}), bf16[16,128,256]{2,1,0:T(8,128)(2,1)}, u32[]{:S(2)}, u32[]{:S(2)}) async-start(bf16[16,128,256]{2,1,0:T(8,128)(2,1)} %get-tuple-element.5), calls=%async_computation.1 | async-start | bytes 2097152 | tf_op jit(solution)/shard_map/all_to_all | solution.py:116
  134.5 28.8 %collective-permute-start.3 = (bf16[16,128,256]{2,1,0:T(8,128)(2,1)S(1)}, bf16[16,128,256]{2,1,0:T(8,128)(2,1)}, u32[]{:S(2)}, u32[]{:S(2)}) collective-permute-start(bf16[16,128,256]{2,1,0:T(8,128)(2,1)S(1)} %all-to-all-done.3.mine_ref), channel_id=1, source_target_pairs={{0,16},{16,0},{1,17},{17,1},{2,18},{18,2},{3,19},{19,3},{4,20},{20... | collective-permute-start | bytes 3145736 | tf_op jit(solution)/shard_map/ppermute | solution.py:117
  135.7 45.7 %collective-permute-start.2 = (bf16[16,128,256]{2,1,0:T(8,128)(2,1)S(1)}, bf16[16,128,256]{2,1,0:T(8,128)(2,1)}, u32[]{:S(2)}, u32[]{:S(2)}) collective-permute-start(bf16[16,128,256]{2,1,0:T(8,128)(2,1)S(1)} %all-to-all-done.2.mine_ref), channel_id=1, source_target_pairs={{0,16},{16,0},{1,17},{17,1},{2,18},{18,2},{3,19},{19,3},{4,20},{20... | collective-permute-start | bytes 3145736 | tf_op jit(solution)/shard_map/ppermute | solution.py:117
  136.0 67.9 %collective-permute-start.1 = (bf16[16,128,256]{2,1,0:T(8,128)(2,1)S(1)}, bf16[16,128,256]{2,1,0:T(8,128)(2,1)}, u32[]{:S(2)}, u32[]{:S(2)}) collective-permute-start(bf16[16,128,256]{2,1,0:T(8,128)(2,1)S(1)} %all-to-all-done.1.mine_ref), channel_id=1, source_target_pairs={{0,16},{16,0},{1,17},{17,1},{2,18},{18,2},{3,19},{19,3},{4,20},{20... | collective-permute-start | bytes 3145736 | tf_op jit(solution)/shard_map/ppermute | solution.py:117
  162.2 64.2 %collective-permute-start = (bf16[16,128,256]{2,1,0:T(8,128)(2,1)}, bf16[16,128,256]{2,1,0:T(8,128)(2,1)}, u32[]{:S(2)}, u32[]{:S(2)}) collective-permute-start(bf16[16,128,256]{2,1,0:T(8,128)(2,1)} %all-to-all-done.mine_ref), channel_id=1, source_target_pairs={{0,16},{16,0},{1,17},{17,1},{2,18},{18,2},{3,19},{19,3},{4,20},{20... | collective-permute-start | bytes 3145736 | tf_op jit(solution)/shard_map/ppermute | solution.py:117
  203.9 34.6 %copy-start.1 = (f32[8,32]{1,0:T(8,128)S(1)}, f32[8,32]{1,0:T(8,128)}, u32[]{:S(2)}) copy-start(f32[8,32]{1,0:T(8,128)} %param.18) | copy-start | bytes 3076
Sparse Core Ops, SparseCore 0:
  10.2 49.4 all-gather.4
  61.8 51.1 all-gather.2
  127.1 62.2 reduce-scatter.1

commit v2 on v1

--- a/solution.py
+++ b/solution.py
@@ -32,26 +32,32 @@
 
 def adam_kernel(tokens, owner_ref, side_ref, hidden_ref, cot_ref, mine_ref, other_ref, *rest):
     out_ref = rest[-1]
+    owners, _, width = mine_ref.shape
     even = side_ref[0] == 0
-    grad = (
-        jnp.dot(hidden_ref[...], cot_ref[...], preferred_element_type=jnp.float32) / tokens
-    )
-    mine = mine_ref[0].astype(jnp.float32)
-    other = other_ref[0].astype(jnp.float32)
-    first = jnp.where(even, mine, other)
-    second = jnp.where(even, other, mine)
-    out_ref[...] = adam(first, second, grad)
-
-
-def adam_chunk(index, chunks, owner_map, side, hidden_t, cot, mine, other, out):
+
+    @pl.loop(0, owners)
+    def _(j):
+        columns = pl.ds(pl.multiple_of(owner_ref[j] * width, width), width)
+        grad = (
+            jnp.dot(hidden_ref[...], cot_ref[:, columns], preferred_element_type=jnp.float32)
+            / tokens
+        )
+        mine = mine_ref[j].astype(jnp.float32)
+        other = other_ref[j].astype(jnp.float32)
+        first = jnp.where(even, mine, other)
+        second = jnp.where(even, other, mine)
+        out_ref[:, columns] = adam(first, second, grad)
+
+
+def adam_chunk(index, owner_map, side, hidden_t, cot, mine, other, out):
     owners, rows, width = mine.shape
     units, tokens = hidden_t.shape
     cols = cot.shape[1]
     in_specs = [
-        pl.BlockSpec((rows, tokens), lambda j, o, s: (index, 0)),
-        pl.BlockSpec((tokens, width), lambda j, o, s: (0, o[j])),
-        pl.BlockSpec((1, rows, width), lambda j, o, s: (j, 0, 0)),
-        pl.BlockSpec((1, rows, width), lambda j, o, s: (j, 0, 0)),
+        pl.BlockSpec((rows, tokens), lambda i, o, s: (index, 0)),
+        pl.BlockSpec((tokens, cols), lambda i, o, s: (0, 0)),
+        pl.BlockSpec((owners, rows, width), lambda i, o, s: (0, 0, 0)),
+        pl.BlockSpec((owners, rows, width), lambda i, o, s: (0, 0, 0)),
     ]
     args = [owner_map, side, hidden_t, cot, mine, other]
     aliases = {}
@@ -63,9 +69,9 @@
         functools.partial(adam_kernel, tokens),
         grid_spec=pltpu.PrefetchScalarGridSpec(
             num_scalar_prefetch=2,
-            grid=(owners,),
+            grid=(1,),
             in_specs=in_specs,
-            out_specs=pl.BlockSpec((rows, width), lambda j, o, s: (index, o[j])),
+            out_specs=pl.BlockSpec((rows, cols), lambda i, o, s: (index, 0)),
         ),
         out_shape=jax.ShapeDtypeStruct((units, cols), jnp.bfloat16),
         input_output_aliases=aliases,
@@ -78,7 +84,204 @@
     )(*args)
 
 
-def body(
+MESH = pl.DeviceIdType.MESH
+LOW = 2
+
+
+def place():
+    group = lax.axis_index("groups")
+    tensor = lax.axis_index("tensor")
+    core = lax.axis_index("dp")
+    high, low = tensor // LOW, lax.rem(tensor, LOW)
+    return group, high, low, core
+
+
+def greet(highs):
+    group, high, low, core = place()
+    barrier = pltpu.get_barrier_semaphore()
+    peers = [(group, lax.rem(high + r, highs) * LOW + low, core) for r in range(1, highs)]
+    peers.append((group, high * LOW + 1 - low, core))
+    peers.append((group, high * LOW + low, 1 - core))
+    for peer in peers:
+        pl.semaphore_signal(barrier, inc=1, device_id=peer, device_id_type=MESH)
+    pl.semaphore_wait(barrier, len(peers))
+
+
+def gather_kernel(highs, x_ref, c_ref, x_out, c_out, send_sem, recv_sem, local_sem):
+    group, high, low, core = place()
+    pairs = ((x_ref, x_out), (c_ref, c_out))
+    block = lambda h, l, k: (h * LOW + l) * 2 + k
+    me = block(high, low, core)
+    greet(highs)
+    started = []
+
+    def push(arr, source, slot, target):
+        copy = pltpu.make_async_remote_copy(
+            src_ref=source,
+            dst_ref=pairs[arr][1].at[slot],
+            send_sem=send_sem.at[len(started)],
+            recv_sem=recv_sem.at[slot, arr],
+            device_id=target,
+            device_id_type=MESH,
+        )
+        copy.start()
+        started.append(copy)
+
+    def arrive(arr, slot):
+        ref = pairs[arr][1].at[slot]
+        pltpu.make_async_remote_copy(
+            src_ref=ref,
+            dst_ref=ref,
+            send_sem=send_sem.at[0],
+            recv_sem=recv_sem.at[slot, arr],
+            device_id=(group, high * LOW + low, 1 - core),
+            device_id_type=MESH,
+        ).wait_recv()
+
+    across = (group, high * LOW + 1 - low, core)
+    sibling = (group, high * LOW + low, 1 - core)
+    locals_ = []
+    for arr, (source, out) in enumerate(pairs):
+        for r in range(1, highs):
+            push(arr, source, me, (group, lax.rem(high + r, highs) * LOW + low, core))
+        push(arr, source, me, across)
+        push(arr, source, me, sibling)
+        keep = pltpu.make_async_copy(source, out.at[me], local_sem.at[arr])
+        keep.start()
+        locals_.append(keep)
+    for arr, (_, out) in enumerate(pairs):
+        for r in range(highs - 1, 0, -1):
+            slot = block(lax.rem(high + r, highs), low, core)
+            arrive(arr, slot)
+            push(arr, out.at[slot], slot, across)
+            push(arr, out.at[slot], slot, sibling)
+        for r in range(highs, 0, -1):
+            slot = block(lax.rem(high + r, highs), 1 - low, core)
+            arrive(arr, slot)
+            push(arr, out.at[slot], slot, sibling)
+    for arr in range(2):
+        for h in range(highs):
+            for l in range(LOW):
+                arrive(arr, block(h, l, 1 - core))
+    for keep in locals_:
+        keep.wait()
+    for copy in started:
+        copy.wait_send()
+
+
+def gather_tokens(x, c):
+    tensor_count = lax.axis_size("tensor")
+    highs = tensor_count // LOW
+    rows, cols = x.shape
+    slots = tensor_count * 2
+    pushes = 2 * (highs + 1 + 2 * (highs - 1) + highs)
+    full = jax.ShapeDtypeStruct((slots, rows, cols), x.dtype)
+    vmem = pl.BlockSpec(memory_space=pltpu.VMEM)
+    x_all, c_all = pl.pallas_call(
+        functools.partial(gather_kernel, highs),
+        out_shape=(full, full),
+        in_specs=[vmem, vmem],
+        out_specs=(vmem, vmem),
+        scratch_shapes=[
+            pltpu.SemaphoreType.DMA((pushes,)),
+            pltpu.SemaphoreType.DMA((slots, 2)),
+            pltpu.SemaphoreType.DMA((2,)),
+        ],
+        compiler_params=pltpu.CompilerParams(collective_id=0, has_side_effects=True),
+        cost_estimate=pl.CostEstimate(flops=0, bytes_accessed=60_000_000, transcendentals=0),
+        name="gather_tokens",
+    )(x, c)
+    return x_all.reshape(slots * rows, cols), c_all.reshape(slots * rows, cols)
+
+
+def scatter_kernel(
+    highs, p_ref, o_ref, got_a, sum_a, got_b, sum_b, got_c,
+    send_a, recv_a, send_b, recv_b, send_c, recv_c,
+):
+    group, high, low, core = place()
+    across = (group, high * LOW + 1 - low, core)
+    sibling = (group, high * LOW + low, 1 - core)
+    greet(highs)
+    add = lambda a, b: (a.astype(jnp.float32) + b.astype(jnp.float32)).astype(jnp.bfloat16)
+
+    def copy_to(source, target_ref, send, recv, target):
+        return pltpu.make_async_remote_copy(
+            src_ref=source,
+            dst_ref=target_ref,
+            send_sem=send,
+            recv_sem=recv,
+            device_id=target,
+            device_id_type=MESH,
+        )
+
+    order = []
+    for l in (1 - low, low):
+        for r in range(1, highs + 1):
+            order.append((lax.rem(high + r, highs), l))
+    first = []
+    for k, (h, l) in enumerate(order):
+        t = h * LOW + l
+        copy = copy_to(p_ref.at[t * 2 + 1 - core], got_a.at[k], send_a.at[k], recv_a.at[k], sibling)
+        copy.start()
+        first.append(copy)
+    second = []
+    for k, (h, l) in enumerate(order):
+        t = h * LOW + l
+        first[k].wait_recv()
+        sum_a[k] = add(p_ref[t * 2 + core], got_a[k])
+        if k < highs:
+            copy = copy_to(sum_a.at[k], got_b.at[k], send_b.at[k], recv_b.at[k], across)
+            copy.start()
+            second.append(copy)
+    third = []
+    for r in range(1, highs + 1):
+        k = r - 1
+        second[k].wait_recv()
+        sum_b[k] = add(sum_a[highs + k], got_b[k])
+        if r < highs:
+            copy = copy_to(
+                sum_b.at[k],
+                got_c.at[k],
+                send_c.at[k],
+                recv_c.at[k],
+                (group, lax.rem(high + r, highs) * LOW + low, core),
+            )
+            copy.start()
+            third.append(copy)
+    total = sum_b[highs - 1].astype(jnp.float32)
+    for k, copy in enumerate(third):
+        copy.wait_recv()
+        total = total + got_c[k].astype(jnp.float32)
+    o_ref[...] = total.astype(jnp.bfloat16)
+    for copy in first + second + third:
+        copy.wait_send()
+
+
+def scatter_sum(partial):
+    tensor_count = lax.axis_size("tensor")
+    highs = tensor_count // LOW
+    slots = tensor_count * 2
+    rows, cols = partial.shape[0] // slots, partial.shape[1]
+    vmem = pl.BlockSpec(memory_space=pltpu.VMEM)
+    buf = lambda count: pltpu.VMEM((count, rows, cols), jnp.bfloat16)
+    sem = pltpu.SemaphoreType.DMA
+    return pl.pallas_call(
+        functools.partial(scatter_kernel, highs),
+        out_shape=jax.ShapeDtypeStruct((rows, cols), jnp.bfloat16),
+        in_specs=[vmem],
+        out_specs=vmem,
+        scratch_shapes=[
+            buf(tensor_count), buf(tensor_count), buf(highs), buf(highs), buf(highs - 1),
+            sem((tensor_count,)), sem((tensor_count,)), sem((highs,)), sem((highs,)),
+            sem((highs - 1,)), sem((highs - 1,)),
+        ],
+        compiler_params=pltpu.CompilerParams(collective_id=1, has_side_effects=True),
+        cost_estimate=pl.CostEstimate(flops=0, bytes_accessed=60_000_000, transcendentals=0),
+        name="scatter_sum",
+    )(partial.reshape(slots, rows, cols))
+
+
+def step_of(
     inputs,
     cotangent,
     gate_blocks,
@@ -101,8 +304,12 @@
     rows = ff // owners
     side = lax.rem(group, 2)
 
-    x_all = lax.all_gather(inputs, TOKENS_AXES, axis=0, tiled=True)
-    cot = lax.all_gather(cotangent, TOKENS_AXES, axis=0, tiled=True)
+    own_kernels = dp_count == 2 and owners <= 16 and owners % 8 == 0 and inputs.shape[0] % 16 == 0
+    if own_kernels:
+        x_all, cot = gather_tokens(inputs, cotangent)
+    else:
+        x_all = lax.all_gather(inputs, TOKENS_AXES, axis=0, tiled=True)
+        cot = lax.all_gather(cotangent, TOKENS_AXES, axis=0, tiled=True)
 
     chunks = CHUNKS if rows % (CHUNKS * 16) == 0 else 1
     step = rows // chunks
@@ -113,8 +320,11 @@
     for c in range(chunks):
         if paired:
             picked = jnp.where(side == 0, shaped_first[:, c], shaped_second[:, c])
+            if c == 1:
+                picked, x_all, cot = lax.optimization_barrier((picked, x_all, cot))
             mine = lax.all_to_all(picked, TOKENS_AXES, split_axis=0, concat_axis=0, tiled=True)
-            received.append((mine, lax.ppermute(mine, "groups", swap)))
+            other = lax.ppermute(mine, "groups", swap)
+            received.append((mine, other))
         else:
             received.append(
                 tuple(
@@ -142,18 +352,18 @@
     nt = (((1,), (1,)), ((), ()))
     partial = lax.dot_general(grad_gate, w_gate, nt, preferred_element_type=jnp.float32)
     partial = partial + lax.dot_general(grad_up, w_up, nt, preferred_element_type=jnp.float32)
-    input_grad = lax.psum_scatter(
-        partial.astype(jnp.bfloat16), TOKENS_AXES, scatter_dimension=0, tiled=True
-    )
+    partial = partial.astype(jnp.bfloat16)
+    if own_kernels:
+        input_grad = scatter_sum(partial)
+    else:
+        input_grad = lax.psum_scatter(partial, TOKENS_AXES, scatter_dimension=0, tiled=True)
 
     hidden_t = hidden.T
     if width % 128 == 0 and step % 16 == 0:
         sides = jnp.full((1,), side if paired else 0, jnp.int32)
         update = None
         for c, (mine, other) in enumerate(received):
-            update = adam_chunk(
-                c, chunks, owner_map, sides, hidden_t, cot, mine, other, update
-            )
+            update = adam_chunk(c, owner_map, sides, hidden_t, cot, mine, other, update)
     else:
         grad = jnp.dot(hidden_t, cot, preferred_element_type=jnp.float32) / cot.shape[0]
         placement = jnp.zeros((owners,), jnp.int32).at[owner_map].set(
@@ -173,8 +383,12 @@
 
 
 def solution(mesh):
+    return step_on(mesh)
+
+
+def step_on(mesh):
     return jax.shard_map(
-        body,
+        step_of,
         mesh=mesh,
         in_specs=(
             P(("groups", "tensor", "dp"), None),

time: 249 us -> 284 us (1.14)
  Pallas kernels: 48.6 us -> 114 us
  waiting for transfers between devices: 111 us -> 66.7 us
  blocking collectives: 0 us -> 31.3 us
  between operations: 13.9 us -> 0.84 us
  starting transfers between devices: 27.2 us -> 21.4 us
    pallas_call x0 -> x2, Pallas kernels: none -> 82.1 us  [the longest x1 58.9 us: gather_tokens(): pl.pallas_call(functools.partial(gather_kernel, highs), out_shape=(full,...]
    all_to_all x4 -> x3, waiting for transfers between devices: 71.2 us -> 21.2 us  [step_of(): lax.all_to_all(picked, TOKENS_AXES, split_axis=0, concat_axis=0, tiled=True)]
    all_to_all x0 -> x1, blocking collectives: none -> 31.3 us  [step_of(): lax.all_to_all(picked, TOKENS_AXES, split_axis=0, concat_axis=0, tiled=True)]
    ppermute x4, waiting for transfers between devices: 26.5 us -> 45.5 us  [step_of(): other = lax.ppermute(mine, 'groups', swap)]
    pallas_call x4, Pallas kernels: 48.6 us -> 31.6 us  [adam_chunk(): pl.pallas_call(functools.partial(adam_kernel, tokens), grid_spec=pltpu.Pr...]
    all_gather x2 -> x0, waiting for transfers between devices: 12.4 us -> none  [the longest x1 12.4 us: body(): cot = lax.all_gather(cotangent, TOKENS_AXES, axis=0, tiled=True)]
    all_to_all x4 -> x3, starting transfers between devices: 23.1 us -> 17.4 us  [step_of(): lax.all_to_all(picked, TOKENS_AXES, split_axis=0, concat_axis=0, tiled=True)]
  transfers between devices with their start and end apart: 11 -> 7, of which waited for: 7 -> 3; matrix products, arithmetic and copies ran while one was open for 17% -> 14% of each run, Pallas kernels for 20% -> 38%
where the time goes in v2:
time: 284 us; the launch traced here: 282 us
  Pallas kernels  114 us (40%)
  waiting for transfers between devices  66.7 us (23%)
  blocking collectives  31.3 us (11%)
  starting transfers between devices  21.4 us (8%)
  matrix products  21.1 us (7%)
  other arithmetic  19.1 us (7%)
  local copies, waits for them, and re-layouts  7.5 us (3%)
    pallas_call x1, Pallas kernels, gather_tokens(): pl.pallas_call(functools.partial(gather_kernel, highs), out_shape=(full,...  58.9 us
    ppermute x4, waiting for transfers between devices, step_of(): other = lax.ppermute(mine, 'groups', swap)  45.5 us
    pallas_call x4, Pallas kernels, adam_chunk(): pl.pallas_call(functools.partial(adam_kernel, tokens), grid_spec=pltpu.Pr...  31.6 us
    all_to_all x1, blocking collectives, step_of(): lax.all_to_all(picked, TOKENS_AXES, split_axis=0, concat_axis=0, tiled=True)  31.3 us
    pallas_call x1, Pallas kernels, scatter_sum(): pl.pallas_call(functools.partial(scatter_kernel, highs), out_shape=jax.Sh...  23.2 us
    all_to_all x3, waiting for transfers between devices, step_of(): lax.all_to_all(picked, TOKENS_AXES, split_axis=0, concat_axis=0, tiled=True)  21.2 us
    all_to_all x3, starting transfers between devices, step_of(): lax.all_to_all(picked, TOKENS_AXES, split_axis=0, concat_axis=0, tiled=True)  17.4 us
    convert_element_type x2, other arithmetic, dequantize(): return scaled.reshape(rows, cols).astype(jnp.bfloat16)  12 us
  transfers between devices with their start and end apart: 7, of which 3 were waited for; matrix products, arithmetic and copies ran while one was open for 14% of the time, Pallas kernels for 38%

profile of v2, /device:TPU:13, one launch (start us, length us, event | category | flops | bytes accessed | tf_op | source)
XLA Modules:
  0.0 281.6 jit_solution(17126956817230423665)
XLA Ops:
  0.6 0.0 copy-start
  0.7 5.2 %fusion.8 = (bf16[16,128,256]{2,1,0:T(8,128)(2,1)}, bf16[16,128,256]{2,1,0:T(8,128)(2,1)}, bf16[16,128,256]{2,1,0:T(8,128)(2,1)S(1)}, bf16[16,128,256]{2,1,0:T(8,128)(2,1)}) fusion(bf16[16,4,128,256]{3,2,1,0:T(8,128)(2,1)} %bitcast.106, bf16[16,4,128,256]{3,2,1,0:T(8,128)(2,1)} %bitcast.107, pred[]{:T(512)S(6)} %eq.2), kind=kLoop, calls=%fused_computation.12 | loop fusion | flops 2097152 | bytes 12582913 | tf_op jit(solution)/shard_map/jit(_where)/select_n | solution.py:322
  5.9 0.0 copy-start.9
  5.9 31.3 %all_to_all.20.mine_ref = bf16[16,128,256]{2,1,0:T(8,128)(2,1)S(1)} all-to-all(bf16[16,128,256]{2,1,0:T(8,128)(2,1)S(1)} %get-tuple-element.14), channel_id=1, replica_groups=mesh['groups'=2,'tensor'=8,'dp'=2] {'tensor','dp'}, dimensions={0} | all-to-all | bytes 2097152 | tf_op jit(solution)/shard_map/all_to_all | solution.py:325
  37.2 4.9 %all-to-all-start.1 = ((bf16[16,128,256]{2,1,0:T(8,128)(2,1)}), bf16[16,128,256]{2,1,0:T(8,128)(2,1)}, u32[]{:S(2)}, u32[]{:S(2)}) async-start(bf16[16,128,256]{2,1,0:T(8,128)(2,1)} %get-tuple-element.13), calls=%async_computation.1 | async-start | bytes 2097152 | tf_op jit(solution)/shard_map/all_to_all | solution.py:325
  42.1 58.9 %gather_tokens.1 = (bf16[16,16,4096]{2,1,0:T(8,128)(2,1)}, bf16[16,16,4096]{2,1,0:T(8,128)(2,1)}) custom-call(bf16[16,4096]{1,0:T(8,128)(2,1)} %x_ref.1, bf16[16,4096]{1,0:T(8,128)(2,1)} %c_ref.1), custom_call_target="tpu_custom_call" | custom-call | bytes 60000000 | tf_op jit(solution)/shard_map/gather_tokens/pallas_call | solution.py:180
  101.0 0.0 all-to-all-done.1.mine_ref
  101.0 7.7 %all-to-all-start.2 = ((bf16[16,128,256]{2,1,0:T(8,128)(2,1)}), bf16[16,128,256]{2,1,0:T(8,128)(2,1)}, u32[]{:S(2)}, u32[]{:S(2)}) async-start(bf16[16,128,256]{2,1,0:T(8,128)(2,1)} %get-tuple-element.11), calls=%async_computation.2 | async-start | bytes 2097152 | tf_op jit(solution)/shard_map/all_to_all | solution.py:325
  108.7 0.0 copy-done.8
  108.7 0.1 copy.23
  108.8 0.1 copy.22
  108.9 1.1 mul.77
  110.0 5.9 %fusion = bf16[4096,512]{1,0:T(8,128)(2,1)} fusion(f32[512,8,4,128]{3,2,1,0:T(4,128)S(1)} %bitcast.102, bf16[4096,1024]{1,0:T(8,128)(2,1)} %param.13, s32[]{:T(128)S(6)} %select_n.45), kind=kLoop, calls=%fused_computation.1 | loop fusion | flops 6291456 | bytes 16777220 | tf_op jit(solution)/shard_map/convert_element_type | solution.py:19
  115.9 17.7 %all-to-all-done.2.mine_ref = bf16[16,128,256]{2,1,0:T(8,128)(2,1)} async-done(((bf16[16,128,256]{2,1,0:T(8,128)(2,1)}), bf16[16,128,256]{2,1,0:T(8,128)(2,1)}, u32[]{:S(2)}, u32[]{:S(2)}) %all-to-all-start.2) | async-done | bytes 1048608 | tf_op jit(solution)/shard_map/all_to_all | solution.py:325
  133.6 4.8 %all-to-all-start.3 = ((bf16[16,128,256]{2,1,0:T(8,128)(2,1)}), bf16[16,128,256]{2,1,0:T(8,128)(2,1)}, u32[]{:S(2)}, u32[]{:S(2)}) async-start(bf16[16,128,256]{2,1,0:T(8,128)(2,1)} %get-tuple-element.12), calls=%async_computation.3 | async-start | bytes 2097152 | tf_op jit(solution)/shard_map/all_to_all | solution.py:325
  138.4 1.1 mul.73
  139.6 0.0 copy-start.3
  139.6 6.1 %fusion.1 = bf16[4096,512]{1,0:T(8,128)(2,1)} fusion(f32[512,8,4,128]{3,2,1,0:T(4,128)S(1)} %bitcast.103, bf16[4096,1024]{1,0:T(8,128)(2,1)} %param.15, s32[]{:T(128)S(6)} %select_n.45), kind=kLoop, calls=%fused_computation.3 | loop fusion | flops 6291456 | bytes 16777220 | tf_op jit(solution)/shard_map/convert_element_type | solution.py:19
  145.7 0.0 copy-done.3
  145.7 0.0 slice-start
  145.7 3.0 %fusion.26 = f32[256,512]{1,0:T(8,128)S(1)} fusion(bf16[256,4096]{1,0:T(8,128)(2,1)} %bitcast.110, bf16[4096,512]{1,0:T(8,128)(2,1)S(1)} %copy-done.3), kind=kOutput, calls=%fused_computation.46 | convolution fusion | flops 1073741824 | bytes 6815744 | tf_op jit(solution)/shard_map/dot_general | solution.py:343
  148.8 0.4 copy-done.10
  149.2 1.2 fusion.25
  150.4 0.0 copy-start.2
  150.4 1.1 mul.70
  151.6 0.2 slice-done.1
  151.8 0.6 copy-done.2
  152.3 5.0 %fusion.4 = f32[256,512]{1,0:T(8,128)S(1)} fusion(bf16[256,4096]{1,0:T(8,128)(2,1)S(1)} %bitcast.101, f32[64,8,32,128]{3,2,1,0:T(8,128)S(1)} %bitcast.104, bf16[1024,4096]{1,0:T(8,128)(2,1)S(1)} %bitcast.109, s32[]{:T(128)S(6)} %select_n.45), kind=kOutput, calls=%fused_computation.8 | convolution fusion | flops 1080033280 | bytes 15204356 | tf_op jit(solution)/shard_map/dot_general | solution.py:347
  157.4 1.3 collective-permute-start
  158.7 0.3 collective-permute-start.1
  158.9 1.2 collective-permute-start.2
  160.1 3.6 %all-to-all-done.3.mine_ref = bf16[16,128,256]{2,1,0:T(8,128)(2,1)} async-done(((bf16[16,128,256]{2,1,0:T(8,128)(2,1)}), bf16[16,128,256]{2,1,0:T(8,128)(2,1)}, u32[]{:S(2)}, u32[]{:S(2)}) %all-to-all-start.3) | async-done | bytes 1048608 | tf_op jit(solution)/shard_map/all_to_all | solution.py:325
  163.7 1.2 collective-permute-start.3
  164.9 5.6 %fusion.19 = f32[256,4096]{1,0:T(8,128)} fusion(bf16[4096,512]{1,0:T(8,128)(2,1)} %fusion, f32[256,512]{1,0:T(8,128)S(1)} %fusion.26, f32[256,512]{1,0:T(8,128)S(1)} %fusion.4, f32[256,512]{1,0:T(8,128)S(1)} %fusion.25), kind=kOutput, calls=%fused_computation.36 | convolution fusion | flops 1075052544 | bytes 9961472 | tf_op jit(solution)/shard_map/dot_general | solution.py:353
  170.5 1.0 copy.25
  171.5 1.0 copy.24
  172.5 6.2 %fusion.3 = bf16[256,4096]{1,0:T(8,128)(2,1)} fusion(f32[256,4096]{1,0:T(8,128)} %fusion.19, bf16[4096,512]{1,0:T(8,128)(2,1)} %fusion.1, f32[256,512]{1,0:T(8,128)S(1)} %fusion.4, f32[256,512]{1,0:T(8,128)S(1)} %fusion.26), kind=kOutput, calls=%fused_computation.7 | convolution fusion | flops 1076625408 | bytes 11534336 | tf_op jit(solution)/shard_map/dot_general | solution.py:354
  178.7 23.2 %scatter_sum.1 = bf16[16,4096]{1,0:T(8,128)(2,1)} custom-call(bf16[16,16,4096]{2,1,0:T(8,128)(2,1)} %bitcast.105), custom_call_target="tpu_custom_call" | custom-call | bytes 60000000 | tf_op jit(solution)/shard_map/scatter_sum/pallas_call | solution.py:268
  201.9 1.9 fusion.15.hidden_ref
  203.8 45.5 %collective-permute-done.3.other_ref = bf16[16,128,256]{2,1,0:T(8,128)(2,1)} collective-permute-done((bf16[16,128,256]{2,1,0:T(8,128)(2,1)}, bf16[16,128,256]{2,1,0:T(8,128)(2,1)}, u32[]{:S(2)}, u32[]{:S(2)}) %collective-permute-start.3) | collective-permute-done | bytes 1048608 | tf_op jit(solution)/shard_map/ppermute | solution.py:326
  249.3 7.8 %adam.4.rest_0_ = bf16[512,4096]{1,0:T(8,128)(2,1)} custom-call(s32[16]{0:T(128)} %owner_ref.7, s32[1]{0:T(128)} %bitcast.6.side_ref, bf16[512,256]{1,0:T(8,128)(2,1)} %fusion.15.hidden_ref, bf16[256,4096]{1,0:T(8,128)(2,1)} %bitcast.97, bf16[16,128,256]{2,1,0:T(8,128)(2,1)} %all-to-all-done.3.mine_ref, bf16[16,128,256]{2,1,0:T(8,128)(2,1)} %collective-permute-done.3.other_ref), custom_call_target="tpu_custom_call" | custom-call | flops 268435456 | bytes 5242880 | tf_op jit(solution)/shard_map/adam/pallas_call | solution.py:68
  257.1 0.0 collective-permute-done.2.other_ref
  257.1 7.8 %adam.5.rest_0_ = bf16[512,4096]{1,0:T(8,128)(2,1)} custom-call(s32[16]{0:T(128)} %owner_ref.7, s32[1]{0:T(128)} %bitcast.6.side_ref, bf16[512,256]{1,0:T(8,128)(2,1)} %fusion.15.hidden_ref, bf16[256,4096]{1,0:T(8,128)(2,1)} %bitcast.98, bf16[16,128,256]{2,1,0:T(8,128)(2,1)} %all-to-all-done.2.mine_ref, ...), custom_call_target="tpu_custom_call", output_to_operand_aliasing={{}: (6, {})} | custom-call | flops 268435456 | bytes 5242880 | tf_op jit(solution)/shard_map/adam/pallas_call | solution.py:68
  265.0 0.0 collective-permute-done.1.other_ref
  265.0 8.0 %adam.6.rest_0_ = bf16[512,4096]{1,0:T(8,128)(2,1)} custom-call(s32[16]{0:T(128)} %owner_ref.7, s32[1]{0:T(128)} %bitcast.6.side_ref, bf16[512,256]{1,0:T(8,128)(2,1)} %fusion.15.hidden_ref, bf16[256,4096]{1,0:T(8,128)(2,1)} %bitcast.99, bf16[16,128,256]{2,1,0:T(8,128)(2,1)} %all-to-all-done.1.mine_ref, ...), custom_call_target="tpu_custom_call", output_to_operand_aliasing={{}: (6, {})} | custom-call | flops 268435456 | bytes 5242880 | tf_op jit(solution)/shard_map/adam/pallas_call | solution.py:68
  272.9 0.0 collective-permute-done.other_ref
  272.9 8.0 %adam.7 = bf16[512,4096]{1,0:T(8,128)(2,1)} custom-call(s32[16]{0:T(128)} %owner_ref.7, s32[1]{0:T(128)} %bitcast.6.side_ref, bf16[512,256]{1,0:T(8,128)(2,1)} %fusion.15.hidden_ref, bf16[256,4096]{1,0:T(8,128)(2,1)} %bitcast.100, bf16[16,128,256]{2,1,0:T(8,128)(2,1)} %copy-done.5, ...), custom_call_target="tpu_custom_call", output_to_operand_aliasing={{}: (6, {})} | custom-call | flops 268435456 | bytes 5242880 | tf_op jit(solution)/shard_map/adam/pallas_call | solution.py:68
  280.9 0.7 copy.51
  (19 shorter events, 0.0 us)
Async XLA Ops:
  0.6 145.0 %copy-start = (f32[8,32]{1,0:T(8,128)S(1)}, f32[8,32]{1,0:T(8,128)}, u32[]{:S(2)}) copy-start(f32[8,32]{1,0:T(8,128)} %param.18) | copy-start | bytes 3076
  5.9 102.8 %copy-start.8 = (f32[32,8]{0,1:T(8,128)S(1)}, f32[32,8]{0,1:T(8,128)}, u32[]{:S(2)}) copy-start(f32[32,8]{0,1:T(8,128)} %param.14) | copy-start | bytes 3076
  5.9 102.8 %copy-start.9 = (f32[32,8]{0,1:T(8,128)S(1)}, f32[32,8]{0,1:T(8,128)}, u32[]{:S(2)}) copy-start(f32[32,8]{0,1:T(8,128)} %param.16) | copy-start | bytes 3076
  37.2 120.2 %copy-start.5 = (bf16[16,128,256]{2,1,0:T(8,128)(2,1)}, bf16[16,128,256]{2,1,0:T(8,128)(2,1)S(1)}, u32[]{:S(2)}) copy-start(bf16[16,128,256]{2,1,0:T(8,128)(2,1)S(1)} %all_to_all.20.mine_ref) | copy-start | bytes 3145732
  37.2 63.8 %all-to-all-start.1 = ((bf16[16,128,256]{2,1,0:T(8,128)(2,1)}), bf16[16,128,256]{2,1,0:T(8,128)(2,1)}, u32[]{:S(2)}, u32[]{:S(2)}) async-start(bf16[16,128,256]{2,1,0:T(8,128)(2,1)} %get-tuple-element.13), calls=%async_computation.1 | async-start | bytes 2097152 | tf_op jit(solution)/shard_map/all_to_all | solution.py:325
  101.0 32.6 %all-to-all-start.2 = ((bf16[16,128,256]{2,1,0:T(8,128)(2,1)}), bf16[16,128,256]{2,1,0:T(8,128)(2,1)}, u32[]{:S(2)}, u32[]{:S(2)}) async-start(bf16[16,128,256]{2,1,0:T(8,128)(2,1)} %get-tuple-element.11), calls=%async_computation.2 | async-start | bytes 2097152 | tf_op jit(solution)/shard_map/all_to_all | solution.py:325
  133.6 30.1 %all-to-all-start.3 = ((bf16[16,128,256]{2,1,0:T(8,128)(2,1)}), bf16[16,128,256]{2,1,0:T(8,128)(2,1)}, u32[]{:S(2)}, u32[]{:S(2)}) async-start(bf16[16,128,256]{2,1,0:T(8,128)(2,1)} %get-tuple-element.12), calls=%async_computation.3 | async-start | bytes 2097152 | tf_op jit(solution)/shard_map/all_to_all | solution.py:325
  139.6 6.1 %copy-start.3 = (bf16[4096,512]{1,0:T(8,128)(2,1)S(1)}, bf16[4096,512]{1,0:T(8,128)(2,1)}, u32[]{:S(2)}) copy-start(bf16[4096,512]{1,0:T(8,128)(2,1)} %fusion) | copy-start | bytes 12582916
  145.7 3.1 %copy-start.4 = (bf16[4096,512]{1,0:T(8,128)(2,1)S(1)}, bf16[4096,512]{1,0:T(8,128)(2,1)}, u32[]{:S(2)}) copy-start(bf16[4096,512]{1,0:T(8,128)(2,1)} %fusion.1) | copy-start | bytes 12582916
  145.7 3.5 %copy-start.10 = (bf16[16,16,4096]{2,1,0:T(8,128)(2,1)S(1)}, bf16[16,16,4096]{2,1,0:T(8,128)(2,1)}, u32[]{:S(2)}) copy-start(bf16[16,16,4096]{2,1,0:T(8,128)(2,1)} %get-tuple-element.7) | copy-start | bytes 6291460
  145.7 5.9 %slice-start = ((s8[8388608]{0:T(1024)(128)(4,1)}), s8[4194304]{0:T(1024)(128)(4,1)S(1)}, s32[]{:S(2)}) async-start(s8[8388608]{0:T(1024)(128)(4,1)} %bitcast.108), calls=%async_computation.4 | async-start | bytes 8388608
  149.2 2.6 slice-start.1
  150.4 1.9 copy-start.2
  157.4 115.5 %collective-permute-start = (bf16[16,128,256]{2,1,0:T(8,128)(2,1)S(1)}, bf16[16,128,256]{2,1,0:T(8,128)(2,1)}, u32[]{:S(2)}, u32[]{:S(2)}) collective-permute-start(bf16[16,128,256]{2,1,0:T(8,128)(2,1)S(1)} %all_to_all.20.mine_ref), channel_id=1, source_target_pairs={{0,16},{16,0},{1,17},{17,1},{2,18},{18,2},{3,19},{19,3},{4,20},{20... | collective-permute-start | bytes 3145736 | tf_op jit(solution)/shard_map/ppermute | solution.py:326
  158.7 106.3 %collective-permute-start.1 = (bf16[16,128,256]{2,1,0:T(8,128)(2,1)}, bf16[16,128,256]{2,1,0:T(8,128)(2,1)}, u32[]{:S(2)}, u32[]{:S(2)}) collective-permute-start(bf16[16,128,256]{2,1,0:T(8,128)(2,1)} %all-to-all-done.1.mine_ref), channel_id=1, source_target_pairs={{0,16},{16,0},{1,17},{17,1},{2,18},{18,2},{3,19},{19,3},{4,20},{20... | collective-permute-start | bytes 3145736 | tf_op jit(solution)/shard_map/ppermute | solution.py:326
  158.9 98.2 %collective-permute-start.2 = (bf16[16,128,256]{2,1,0:T(8,128)(2,1)}, bf16[16,128,256]{2,1,0:T(8,128)(2,1)}, u32[]{:S(2)}, u32[]{:S(2)}) collective-permute-start(bf16[16,128,256]{2,1,0:T(8,128)(2,1)} %all-to-all-done.2.mine_ref), channel_id=1, source_target_pairs={{0,16},{16,0},{1,17},{17,1},{2,18},{18,2},{3,19},{19,3},{4,20},{20... | collective-permute-start | bytes 3145736 | tf_op jit(solution)/shard_map/ppermute | solution.py:326
  163.7 85.6 %collective-permute-start.3 = (bf16[16,128,256]{2,1,0:T(8,128)(2,1)}, bf16[16,128,256]{2,1,0:T(8,128)(2,1)}, u32[]{:S(2)}, u32[]{:S(2)}) collective-permute-start(bf16[16,128,256]{2,1,0:T(8,128)(2,1)} %all-to-all-done.3.mine_ref), channel_id=1, source_target_pairs={{0,16},{16,0},{1,17},{17,1},{2,18},{18,2},{3,19},{19,3},{4,20},{20... | collective-permute-start | bytes 3145736 | tf_op jit(solution)/shard_map/ppermute | solution.py:326
  172.5 29.4 %copy-start.6 = (f32[256,512]{0,1:T(8,128)S(1)}, f32[256,512]{0,1:T(8,128)}, u32[]{:S(2)}) copy-start(f32[256,512]{0,1:T(8,128)} %copy.25) | copy-start | bytes 1572868
  265.0 16.6 %copy-start.1 = (f32[8,32]{1,0:T(8,128)S(1)}, f32[8,32]{1,0:T(8,128)}, u32[]{:S(2)}) copy-start(f32[8,32]{1,0:T(8,128)} %param.18) | copy-start | bytes 3076
  272.9 8.0 %copy-start.7 = (bf16[16,4096]{1,0:T(8,128)(2,1)S(1)}, bf16[16,4096]{1,0:T(8,128)(2,1)}, u32[]{:S(2)}) copy-start(bf16[16,4096]{1,0:T(8,128)(2,1)} %scatter_sum.1) | copy-start | bytes 393220
